TPU v7x, 32 devices: a whole 2x2x4 slice. The times are simulated.
32 devices in a mesh: worker: 4 (over x, core), outer: 4 (over z), mp: 2 (over y).
Axes of the slice: x: 2, y: 2, z: 4, core: 2. Of those that a mesh axis runs over, the one named last changes fastest.
Arguments:
- grads: float32 [4, 4, 3584, 4096], P('worker', 'outer', None, 'mp'), as said below
- center: float32 [3584, 4096], P(('worker', 'outer'), 'mp'), may hold values from -6 to 6
- radius: float32 [1], replicated, may hold values from 1.5 to 3.5
Outputs:
- center_out: float32 [3584, 4096], P(('worker', 'outer'), 'mp')
Inputs may be any that keep to these rules, and one draw needn't show every extreme that they name: `grads`: finite values.
All inputs are finite; a program needn't handle non-finite values.
Results may differ from a plain program's by a relative error of at most 0.0001.
Values sent between devices are 32-bit elements; how exact they have to be, the bound alone decides.
No kernel may reach another device: no remote copies, remote signals or barrier semaphores. Data moves between devices by JAX's collectives and lax.ppermute only.
A program may use at most 192 MiB of HBM per device.

v0:
```python
import math
import jax
import jax.numpy as jnp
from jax import lax
from jax.sharding import PartitionSpec as P

D = 3584
ITERS = 2
KVW = 4096
epsilon = 1e-06


def on_device(grads, center, radius):
    worker_count = lax.axis_size("worker") * lax.axis_size("outer")
    radius_total = radius[0] * math.sqrt(D * KVW)
    own_rows = center
    mine = grads.reshape(1, grads.shape[2], grads.shape[3])
    gathered = lax.all_to_all(mine, ("worker", "outer"), split_axis=1, concat_axis=0, tiled=True)
    for iteration in range(ITERS):
        difference = gathered - own_rows[None]
        partial_value = jnp.sum(difference * difference, axis=(1, 2))
        norm_sq = lax.psum(partial_value, ("worker", "outer", "mp"))
        factor = jnp.minimum(1.0, radius_total * lax.rsqrt(norm_sq + epsilon))
        summed = jnp.sum(factor[:, None, None] * difference, axis=0)
        own_rows = own_rows + summed / worker_count
    return own_rows


def solution(mesh):
    in_specs = (P("worker", "outer", None, "mp"), P(("worker", "outer"), "mp"), P())
    out_specs = P(("worker", "outer"), "mp")
    return jax.shard_map(
        on_device, mesh=mesh, in_specs=in_specs, out_specs=out_specs, check_vma=False
    )
```

profile of v0, /device:TPU:0, one launch (start us, length us, event | category | flops | bytes accessed | tf_op | source)
XLA Modules:
  0.0 934.4 jit_solution(12065390304282626729)
XLA Ops:
  0.0 23.7 %reshape.36 = f32[1,3584,2048]{2,0,1:T(1,128)} reshape(f32[1,1,3584,2048]{3,2,1,0:T(8,128)} %param.3) | data formatting | bytes 58720256 | tf_op jit(solution)/shard_map/reshape | solution.py:17
  23.7 0.0 copy-start.1
  23.7 7.6 all-to-all-start
  31.9 0.0 copy-done.1
  31.9 10.4 %sub.34 = f32[16,224,2048]{2,1,0:T(8,128)} broadcast(f32[224,2048]{1,0:T(8,128)S(1)} %copy-done.1), dimensions={1,2} | broadcast | bytes 31195136 | tf_op jit(solution)/shard_map/sub | solution.py:20
  42.3 42.5 %sub.35 = f32[1,3584,2048]{2,0,1:T(1,128)} reshape(f32[16,224,2048]{2,1,0:T(8,128)} %sub.34) | data formatting | bytes 58720256 | tf_op jit(solution)/shard_map/sub | solution.py:20
  84.8 580.0 %all-to-all-done = f32[1,3584,2048]{2,0,1:T(1,128)} async-done(((f32[1,3584,2048]{2,0,1:T(1,128)}), f32[1,3584,2048]{2,0,1:T(1,128)}, u32[]{:S(2)}, u32[]{:S(2)}) %all-to-all-start) | async-done | bytes 29360160 | tf_op jit(solution)/shard_map/all_to_all | solution.py:18
  664.9 45.4 %multiply_reduce_fusion.3 = f32[3584]{0:T(1024)S(1)} fusion(f32[1,3584,2048]{2,0,1:T(1,128)} %all-to-all-done, f32[1,3584,2048]{2,0,1:T(1,128)} %sub.35), kind=kLoop, calls=%fused_computation.3 | loop fusion | flops 22016512 | bytes 58734592 | tf_op jit(solution)/shard_map/reduce_sum | solution.py:21
  710.3 0.1 reduce_sum.43
  710.4 0.1 reduce_sum.52
  710.5 37.4 %psum.14 = f32[16]{0:T(128)S(1)} all-reduce(f32[16]{0:T(128)S(1)} %reduce_sum.52), channel_id=1, replica_groups=mesh['worker'=4,'outer'=4,'mp'=2] {'worker','outer','mp'}, use_global_device_ids=true, to_apply=%region_2.0 | all-reduce | flops 16 | bytes 128 | tf_op jit(solution)/shard_map/psum | solution.py:22
  747.9 17.7 %copy.4 = f32[1,3584,2048]{2,1,0:T(8,128)S(1)} copy(f32[1,3584,2048]{2,0,1:T(1,128)} %all-to-all-done) | data formatting | bytes 58720256
  765.6 0.0 copy-start
  765.6 0.0 copy-start.2
  765.6 10.3 %copy-done = f32[1,3584,2048]{2,1,0:T(8,128)} copy-done((f32[1,3584,2048]{2,1,0:T(8,128)}, f32[1,3584,2048]{2,1,0:T(8,128)S(1)}, u32[]{:S(2)}) %copy-start) | copy-done | bytes 29360152
  775.9 4.4 multiply_reduce_fusion.2
  780.3 0.0 copy-done.2
  780.3 0.3 multiply_add_fusion.1
  780.6 10.4 %sub.38 = f32[16,224,2048]{2,1,0:T(8,128)} broadcast(f32[224,2048]{1,0:T(8,128)S(1)} %multiply_add_fusion.1), dimensions={1,2} | broadcast | bytes 31195136 | tf_op jit(solution)/shard_map/sub | solution.py:20
  791.0 42.5 %sub.39 = f32[1,3584,2048]{2,0,1:T(1,128)} reshape(f32[16,224,2048]{2,1,0:T(8,128)} %sub.38) | data formatting | bytes 58720256 | tf_op jit(solution)/shard_map/sub | solution.py:20
  833.6 45.4 %multiply_reduce_fusion.1 = f32[3584]{0:T(1024)S(1)} fusion(f32[1,3584,2048]{2,0,1:T(1,128)} %all-to-all-done, f32[1,3584,2048]{2,0,1:T(1,128)} %sub.39), kind=kLoop, calls=%fused_computation.1 | loop fusion | flops 22016512 | bytes 58734592 | tf_op jit(solution)/shard_map/reduce_sum | solution.py:21
  879.0 0.1 reduce_sum.55
  879.0 0.1 reduce_sum.56
  879.2 41.8 %psum.15 = f32[16]{0:T(128)S(1)} all-reduce(f32[16]{0:T(128)S(1)} %reduce_sum.56), channel_id=1, replica_groups=mesh['worker'=4,'outer'=4,'mp'=2] {'worker','outer','mp'}, use_global_device_ids=true, to_apply=%region_6.7 | all-reduce | flops 16 | bytes 128 | tf_op jit(solution)/shard_map/psum | solution.py:22
  920.9 11.9 %multiply_reduce_fusion = f32[224,2048]{1,0:T(8,128)S(1)} fusion(f32[16,224,2048]{2,1,0:T(8,128)} %bitcast.5, f32[16]{0:T(128)S(1)} %multiply_minimum_fusion, f32[224,2048]{1,0:T(8,128)S(1)} %multiply_add_fusion.1), kind=kLoop, calls=%fused_computation | loop fusion | flops 21561344 | bytes 33030208 | tf_op jit(solution)/shard_map/reduce_sum | solution.py:24
  932.8 1.5 multiply_add_fusion
  (2 shorter events, 0.0 us)
Async XLA Ops:
  23.7 8.2 copy-start.1
  23.7 641.2 %all-to-all-start = ((f32[1,3584,2048]{2,0,1:T(1,128)}), f32[1,3584,2048]{2,0,1:T(1,128)}, u32[]{:S(2)}, u32[]{:S(2)}) async-start(f32[1,3584,2048]{2,0,1:T(1,128)} %reshape.36), calls=%async_computation | async-start | bytes 58720256 | tf_op jit(solution)/shard_map/all_to_all | solution.py:18
  765.6 10.3 %copy-start = (f32[1,3584,2048]{2,1,0:T(8,128)}, f32[1,3584,2048]{2,1,0:T(8,128)S(1)}, u32[]{:S(2)}) copy-start(f32[1,3584,2048]{2,1,0:T(8,128)S(1)} %copy.4) | copy-start | bytes 88080384
  765.6 14.7 %copy-start.2 = (f32[224,2048]{1,0:T(8,128)S(1)}, f32[224,2048]{1,0:T(8,128)}, u32[]{:S(2)}) copy-start(f32[224,2048]{1,0:T(8,128)} %param.4) | copy-start | bytes 5505028
where the time goes:
time: 937 us; the launch traced here: 934 us
  waiting for transfers between devices  580 us (62%)
  local copies, waits for them, and re-layouts  158 us (17%)
  other arithmetic  109 us (12%)
  blocking collectives  79.2 us (8%)
    all_to_all x1, waiting for transfers between devices, on_device(): lax.all_to_all(mine, ('worker', 'outer'), split_axis=1, concat_axis=0, ti...  580 us
    sub x4, local copies, waits for them, and re-layouts, on_device(): difference = gathered - own_rows[None]  106 us
    reduce_sum x4, other arithmetic, on_device(): partial_value = jnp.sum(difference * difference, axis=(1, 2))  91.1 us
    psum x2, blocking collectives, on_device(): norm_sq = lax.psum(partial_value, ('worker', 'outer', 'mp'))  79.2 us
    unnamed x7, local copies, waits for them, and re-layouts  28 us
    reshape x1, local copies, waits for them, and re-layouts, on_device(): mine = grads.reshape(1, grads.shape[2], grads.shape[3])  23.7 us
  transfers between devices with their start and end apart: 1, of which 1 were waited for; matrix products, arithmetic and copies ran while one was open for 6% of the time, Pallas kernels for 0%

commit v1 on v0

--- a/solution.py
+++ b/solution.py
@@ -15,7 +15,15 @@
     radius_total = radius[0] * math.sqrt(D * KVW)
     own_rows = center
     mine = grads.reshape(1, grads.shape[2], grads.shape[3])
-    gathered = lax.all_to_all(mine, ("worker", "outer"), split_axis=1, concat_axis=0, tiled=True)
+    gathered = jnp.concatenate(
+        lax.all_to_all(
+            jnp.stack(jnp.split(mine, lax.axis_size(("worker", "outer")), axis=1)),
+            ("worker", "outer"),
+            0,
+            0,
+        ),
+        axis=0,
+    )
     for iteration in range(ITERS):
         difference = gathered - own_rows[None]
         partial_value = jnp.sum(difference * difference, axis=(1, 2))

time: 937 us -> 807 us (0.86)
  local copies, waits for them, and re-layouts: 158 us -> 37.5 us
  other arithmetic: 109 us -> 48.9 us
  waiting for transfers between devices: 580 us -> 633 us
    sub x4 -> x0, local copies, waits for them, and re-layouts: 106 us -> none  [on_device(): difference = gathered - own_rows[None]]
    reduce_sum x4 -> x2, other arithmetic: 91.1 us -> 23.2 us  [on_device(): partial_value = jnp.sum(difference * difference, axis=(1, 2))]
    all_to_all x1, waiting for transfers between devices: 580 us -> 633 us  [on_device(): lax.all_to_all(jnp.stack(jnp.split(mine, lax.axis_size(('worker', 'outer'...]
    reshape x1 -> x0, local copies, waits for them, and re-layouts: 23.7 us -> none  [on_device(): mine = grads.reshape(1, grads.shape[2], grads.shape[3])]
    unnamed x7 -> x21, local copies, waits for them, and re-layouts: 28 us -> 36.1 us
  transfers between devices with their start and end apart: 1 -> 1, of which waited for: 1 -> 1; matrix products, arithmetic and copies ran while one was open for 6% -> 0% of each run, Pallas kernels for 0% -> 0%
where the time goes in v1:
time: 807 us
  waiting for transfers between devices  633 us (78%)
  blocking collectives  79.1 us (10%)
  other arithmetic  48.9 us (6%)
  local copies, waits for them, and re-layouts  37.5 us (5%)
    all_to_all x1, waiting for transfers between devices, on_device(): lax.all_to_all(jnp.stack(jnp.split(mine, lax.axis_size(('worker', 'outer'...  633 us
    psum x2, blocking collectives, on_device(): norm_sq = lax.psum(partial_value, ('worker', 'outer', 'mp'))  79.1 us
    unnamed x21, local copies, waits for them, and re-layouts  36.1 us
    reduce_sum x2, other arithmetic, on_device(): summed = jnp.sum(factor[:, None, None] * difference, axis=0)  23.9 us
    reduce_sum x2, other arithmetic, on_device(): partial_value = jnp.sum(difference * difference, axis=(1, 2))  23.2 us
  transfers between devices with their start and end apart: 1, of which 1 were waited for; matrix products, arithmetic and copies ran while one was open for 0% of the time, Pallas kernels for 0%

profile of v1, /device:TPU:0, one launch (start us, length us, event | category | flops | bytes accessed | tf_op | source)
XLA Modules:
  0.0 806.7 jit_solution(8485957217396782042)
XLA Ops:
  0.0 0.0 copy-start
  0.0 3.1 fusion.15
  3.1 3.7 fusion.14
  6.8 3.7 fusion.13
  10.5 3.7 fusion.12
  14.2 3.0 fusion.11
  17.2 2.9 fusion.10
  20.1 3.0 fusion.9
  23.0 3.0 fusion.8
  26.0 0.0 copy-done
  26.0 1.4 fusion.7
  27.4 1.5 fusion.6
  28.9 1.4 fusion.5
  30.3 1.4 fusion.4
  31.7 1.4 fusion.3
  33.2 1.5 fusion.2
  34.6 1.4 fusion.1
  36.1 1.4 fusion
  37.5 0.0 copy-start.1
  37.5 7.6 all-to-all-start
  45.7 633.0 %all-to-all-done = f32[16,1,224,2048]{3,2,1,0:T(8,128)} async-done(((f32[16,1,224,2048]{3,2,1,0:T(8,128)}), f32[16,1,224,2048]{3,2,1,0:T(8,128)}, u32[]{:S(2)}, u32[]{:S(2)}) %all-to-all-start) | async-done | bytes 29360160 | tf_op jit(solution)/shard_map/all_to_all | solution.py:19
  678.7 0.0 copy-done.1
  678.7 11.6 %multiply_reduce_fusion.3 = f32[16]{0:T(128)S(1)} fusion(f32[16,1,224,2048]{3,2,1,0:T(8,128)} %all-to-all-done, f32[224,2048]{1,0:T(8,128)S(1)} %copy-done.1), kind=kLoop, calls=%fused_computation.5 | loop fusion | flops 22020080 | bytes 31195200 | tf_op jit(solution)/shard_map/reduce_sum | solution.py:29
  690.3 37.4 %psum.14 = f32[16]{0:T(128)S(1)} all-reduce(f32[16]{0:T(128)S(1)} %multiply_reduce_fusion.3), channel_id=1, replica_groups=mesh['worker'=4,'outer'=4,'mp'=2] {'worker','outer','mp'}, use_global_device_ids=true, to_apply=%region_1.0 | all-reduce | flops 16 | bytes 128 | tf_op jit(solution)/shard_map/psum | solution.py:30
  727.7 0.0 copy-start.2
  727.7 12.0 %multiply_reduce_fusion.2 = f32[224,2048]{1,0:T(8,128)S(1)} fusion(f32[16,1,224,2048]{3,2,1,0:T(8,128)} %all-to-all-done, f32[16]{0:T(128)S(1)} %multiply_minimum_fusion.1, f32[224,2048]{1,0:T(8,128)S(1)} %copy-done.1), kind=kLoop, calls=%fused_computation.4 | loop fusion | flops 21561344 | bytes 33030208 | tf_op jit(solution)/shard_map/reduce_sum | solution.py:32
  739.7 0.0 copy-done.2
  739.7 0.2 multiply_add_fusion.1
  739.9 11.6 %multiply_reduce_fusion.1 = f32[16]{0:T(128)S(1)} fusion(f32[16,1,224,2048]{3,2,1,0:T(8,128)} %all-to-all-done, f32[224,2048]{1,0:T(8,128)S(1)} %multiply_add_fusion.1), kind=kLoop, calls=%fused_computation.3 | loop fusion | flops 22020080 | bytes 31195200 | tf_op jit(solution)/shard_map/reduce_sum | solution.py:29
  751.5 41.7 %psum.15 = f32[16]{0:T(128)S(1)} all-reduce(f32[16]{0:T(128)S(1)} %multiply_reduce_fusion.1), channel_id=1, replica_groups=mesh['worker'=4,'outer'=4,'mp'=2] {'worker','outer','mp'}, use_global_device_ids=true, to_apply=%region_4.0 | all-reduce | flops 16 | bytes 128 | tf_op jit(solution)/shard_map/psum | solution.py:30
  793.3 11.9 %multiply_reduce_fusion = f32[224,2048]{1,0:T(8,128)S(1)} fusion(f32[16,1,224,2048]{3,2,1,0:T(8,128)} %all-to-all-done, f32[16]{0:T(128)S(1)} %multiply_minimum_fusion, f32[224,2048]{1,0:T(8,128)S(1)} %multiply_add_fusion.1), kind=kLoop, calls=%fused_computation.2 | loop fusion | flops 21561344 | bytes 33030208 | tf_op jit(solution)/shard_map/reduce_sum | solution.py:32
  805.2 1.5 multiply_add_fusion
  (2 shorter events, 0.0 us)
Async XLA Ops:
  0.0 26.0 %copy-start = (f32[1,1,3584,2048]{3,2,1,0:T(8,128)S(1)}, f32[1,1,3584,2048]{3,2,1,0:T(8,128)}, u32[]{:S(2)}) copy-start(f32[1,1,3584,2048]{3,2,1,0:T(8,128)} %param.3) | copy-start | bytes 88080384
  37.5 641.2 %copy-start.1 = (f32[224,2048]{1,0:T(8,128)S(1)}, f32[224,2048]{1,0:T(8,128)}, u32[]{:S(2)}) copy-start(f32[224,2048]{1,0:T(8,128)} %param.4) | copy-start | bytes 5505028
  37.5 641.2 %all-to-all-start = ((f32[16,1,224,2048]{3,2,1,0:T(8,128)}), f32[16,1,224,2048]{3,2,1,0:T(8,128)}, u32[]{:S(2)}, u32[]{:S(2)}) async-start(f32[16,1,224,2048]{3,2,1,0:T(8,128)} %fusion), calls=%async_computation | async-start | bytes 58720256 | tf_op jit(solution)/shard_map/all_to_all | solution.py:19
  727.7 12.0 %copy-start.2 = (f32[224,2048]{1,0:T(8,128)S(1)}, f32[224,2048]{1,0:T(8,128)}, u32[]{:S(2)}) copy-start(f32[224,2048]{1,0:T(8,128)} %param.4) | copy-start | bytes 5505028

commit v2 on v0

--- a/solution.py
+++ b/solution.py
@@ -19,7 +19,7 @@
     for iteration in range(ITERS):
         difference = gathered - own_rows[None]
         partial_value = jnp.sum(difference * difference, axis=(1, 2))
-        norm_sq = lax.psum(partial_value, ("worker", "outer", "mp"))
+        norm_sq = lax.psum(lax.psum(partial_value, "worker"), ("outer", "mp"))
         factor = jnp.minimum(1.0, radius_total * lax.rsqrt(norm_sq + epsilon))
         summed = jnp.sum(factor[:, None, None] * difference, axis=0)
         own_rows = own_rows + summed / worker_count

time: 937 us -> 907 us (0.968)
  blocking collectives: 79.2 us -> 48.9 us
    psum x2 -> x4, blocking collectives: 79.2 us -> 48.9 us  [on_device(): norm_sq = lax.psum(lax.psum(partial_value, 'worker'), ('outer', 'mp'))]
where the time goes in v2:
time: 907 us; the launch traced here: 904 us
  waiting for transfers between devices  580 us (64%)
  local copies, waits for them, and re-layouts  158 us (17%)
  other arithmetic  109 us (12%)
  blocking collectives  48.9 us (5%)
    all_to_all x1, waiting for transfers between devices, on_device(): lax.all_to_all(mine, ('worker', 'outer'), split_axis=1, concat_axis=0, ti...  580 us
    sub x4, local copies, waits for them, and re-layouts, on_device(): difference = gathered - own_rows[None]  106 us
    reduce_sum x4, other arithmetic, on_device(): partial_value = jnp.sum(difference * difference, axis=(1, 2))  91.1 us
    psum x4, blocking collectives, on_device(): norm_sq = lax.psum(lax.psum(partial_value, 'worker'), ('outer', 'mp'))  48.9 us
    unnamed x7, local copies, waits for them, and re-layouts  28 us
    reshape x1, local copies, waits for them, and re-layouts, on_device(): mine = grads.reshape(1, grads.shape[2], grads.shape[3])  23.7 us
  transfers between devices with their start and end apart: 1, of which 1 were waited for; matrix products, arithmetic and copies ran while one was open for 6% of the time, Pallas kernels for 0%

profile of v2, /device:TPU:0, one launch (start us, length us, event | category | flops | bytes accessed | tf_op | source)
XLA Modules:
  0.0 904.1 jit_solution(15798235343436848863)
XLA Ops:
  0.0 23.7 %reshape.36 = f32[1,3584,2048]{2,0,1:T(1,128)} reshape(f32[1,1,3584,2048]{3,2,1,0:T(8,128)} %param.3) | data formatting | bytes 58720256 | tf_op jit(solution)/shard_map/reshape | solution.py:17
  23.7 0.0 copy-start.1
  23.7 7.6 all-to-all-start
  31.9 0.0 copy-done.1
  31.9 10.4 %sub.34 = f32[16,224,2048]{2,1,0:T(8,128)} broadcast(f32[224,2048]{1,0:T(8,128)S(1)} %copy-done.1), dimensions={1,2} | broadcast | bytes 31195136 | tf_op jit(solution)/shard_map/sub | solution.py:20
  42.3 42.5 %sub.35 = f32[1,3584,2048]{2,0,1:T(1,128)} reshape(f32[16,224,2048]{2,1,0:T(8,128)} %sub.34) | data formatting | bytes 58720256 | tf_op jit(solution)/shard_map/sub | solution.py:20
  84.8 580.0 %all-to-all-done = f32[1,3584,2048]{2,0,1:T(1,128)} async-done(((f32[1,3584,2048]{2,0,1:T(1,128)}), f32[1,3584,2048]{2,0,1:T(1,128)}, u32[]{:S(2)}, u32[]{:S(2)}) %all-to-all-start) | async-done | bytes 29360160 | tf_op jit(solution)/shard_map/all_to_all | solution.py:18
  664.9 45.4 %multiply_reduce_fusion.3 = f32[3584]{0:T(1024)S(1)} fusion(f32[1,3584,2048]{2,0,1:T(1,128)} %all-to-all-done, f32[1,3584,2048]{2,0,1:T(1,128)} %sub.35), kind=kLoop, calls=%fused_computation.3 | loop fusion | flops 22016512 | bytes 58734592 | tf_op jit(solution)/shard_map/reduce_sum | solution.py:21
  710.3 0.1 reduce_sum.43
  710.4 0.1 reduce_sum.52
  710.5 6.2 psum.28
  716.7 19.8 %psum.29 = f32[16]{0:T(128)S(1)} all-reduce(f32[16]{0:T(128)S(1)} %psum.28), channel_id=1, replica_groups=mesh['worker'=4,'outer'=4,'mp'=2] {'outer','mp'}, use_global_device_ids=true, to_apply=%region_3.0 | all-reduce | flops 16 | bytes 128 | tf_op jit(solution)/shard_map/psum | solution.py:22
  736.5 17.7 %copy.4 = f32[1,3584,2048]{2,1,0:T(8,128)S(1)} copy(f32[1,3584,2048]{2,0,1:T(1,128)} %all-to-all-done) | data formatting | bytes 58720256
  754.2 0.0 copy-start
  754.2 0.0 copy-start.2
  754.2 10.3 %copy-done = f32[1,3584,2048]{2,1,0:T(8,128)} copy-done((f32[1,3584,2048]{2,1,0:T(8,128)}, f32[1,3584,2048]{2,1,0:T(8,128)S(1)}, u32[]{:S(2)}) %copy-start) | copy-done | bytes 29360152
  764.6 4.4 multiply_reduce_fusion.2
  768.9 0.0 copy-done.2
  768.9 0.3 multiply_add_fusion.1
  769.3 10.4 %sub.38 = f32[16,224,2048]{2,1,0:T(8,128)} broadcast(f32[224,2048]{1,0:T(8,128)S(1)} %multiply_add_fusion.1), dimensions={1,2} | broadcast | bytes 31195136 | tf_op jit(solution)/shard_map/sub | solution.py:20
  779.6 42.5 %sub.39 = f32[1,3584,2048]{2,0,1:T(1,128)} reshape(f32[16,224,2048]{2,1,0:T(8,128)} %sub.38) | data formatting | bytes 58720256 | tf_op jit(solution)/shard_map/sub | solution.py:20
  822.2 45.4 %multiply_reduce_fusion.1 = f32[3584]{0:T(1024)S(1)} fusion(f32[1,3584,2048]{2,0,1:T(1,128)} %all-to-all-done, f32[1,3584,2048]{2,0,1:T(1,128)} %sub.39), kind=kLoop, calls=%fused_computation.1 | loop fusion | flops 22016512 | bytes 58734592 | tf_op jit(solution)/shard_map/reduce_sum | solution.py:21
  867.6 0.1 reduce_sum.55
  867.7 0.1 reduce_sum.56
  867.8 5.8 psum.30
  873.6 17.1 %psum.31 = f32[16]{0:T(128)S(1)} all-reduce(f32[16]{0:T(128)S(1)} %psum.30), channel_id=1, replica_groups=mesh['worker'=4,'outer'=4,'mp'=2] {'outer','mp'}, use_global_device_ids=true, to_apply=%region_8.9 | all-reduce | flops 16 | bytes 128 | tf_op jit(solution)/shard_map/psum | solution.py:22
  890.7 11.9 %multiply_reduce_fusion = f32[224,2048]{1,0:T(8,128)S(1)} fusion(f32[16,224,2048]{2,1,0:T(8,128)} %bitcast.5, f32[16]{0:T(128)S(1)} %multiply_minimum_fusion, f32[224,2048]{1,0:T(8,128)S(1)} %multiply_add_fusion.1), kind=kLoop, calls=%fused_computation | loop fusion | flops 21561344 | bytes 33030208 | tf_op jit(solution)/shard_map/reduce_sum | solution.py:24
  902.6 1.5 multiply_add_fusion
  (2 shorter events, 0.0 us)
Async XLA Ops:
  23.7 8.2 copy-start.1
  23.7 641.2 %all-to-all-start = ((f32[1,3584,2048]{2,0,1:T(1,128)}), f32[1,3584,2048]{2,0,1:T(1,128)}, u32[]{:S(2)}, u32[]{:S(2)}) async-start(f32[1,3584,2048]{2,0,1:T(1,128)} %reshape.36), calls=%async_computation | async-start | bytes 58720256 | tf_op jit(solution)/shard_map/all_to_all | solution.py:18
  754.2 10.3 %copy-start = (f32[1,3584,2048]{2,1,0:T(8,128)}, f32[1,3584,2048]{2,1,0:T(8,128)S(1)}, u32[]{:S(2)}) copy-start(f32[1,3584,2048]{2,1,0:T(8,128)S(1)} %copy.4) | copy-start | bytes 88080384
  754.2 14.7 %copy-start.2 = (f32[224,2048]{1,0:T(8,128)S(1)}, f32[224,2048]{1,0:T(8,128)}, u32[]{:S(2)}) copy-start(f32[224,2048]{1,0:T(8,128)} %param.4) | copy-start | bytes 5505028
